TPU v7x, 512 devices: a whole 4x4x16 slice. The times are simulated.
512 devices in a mesh: ctx: 64 (over z, x), ch: 8 (over y, core).
Axes of the slice: x: 4, y: 4, z: 16, core: 2. Of those that a mesh axis runs over, the one named last changes fastest.
Arguments:
- gate_input: bfloat16 [16384, 4096], P('ctx', 'ch'), may hold values from -6 to 6
- key_input: bfloat16 [16384, 4096], P('ctx', 'ch'), may hold values from -6 to 6
- value_input: bfloat16 [16384, 4096], P('ctx', 'ch'), may hold values from -6 to 6
- decay_rate: float32 [16, 4096], P(None, 'ch'), may hold values from 0.00012207031 to 0.26666667
- frequency: float32 [16, 4096], P(None, 'ch'), may hold values from 0 to 2.4
- residue: float32 [2, 16, 4096], P(None, None, 'ch'), may hold values from -2 to 2
- skip_gain: float32 [4096], P('ch'), may hold values from -3 to 3
- out_weight: bfloat16 [4096, 4096], P('ctx', 'ch'), may hold values from -0.09375 to 0.09375
Outputs:
- mixed: bfloat16 [16384, 4096], P('ctx', 'ch')
All inputs are finite; a program needn't handle non-finite values.
Results may differ from a plain program's by a relative error of at most 0.014.
Values may be sent and summed in bfloat16 or wider, within the bound.
A program may use at most 128 MiB of HBM per device.

v0:
```python
import jax
import jax.numpy as jnp
from jax import lax
from jax.sharding import PartitionSpec as P


def entering(value, axis, join, neutral):
    count, mine = (lax.axis_size(axis), lax.axis_index(axis))
    pieces = jax.tree.map(lambda part: lax.all_gather(part, axis), value)
    so_far = jax.tree.map(
        lambda part, zero: jnp.full_like(part, 0) + jnp.asarray(zero, part.dtype), value, neutral
    )

    def hop(position, so_far):
        longer = join(so_far, jax.tree.map(lambda part: part[position], pieces))
        return jax.tree.map(lambda new, old: jnp.where(position < mine, new, old), longer, so_far)

    return lax.fori_loop(0, count - 1, hop, so_far)


def cmul(a_re, a_im, b_re, b_im):
    return (a_re * b_re - a_im * b_im, a_re * b_im + a_im * b_re)


def filter_tables(decay_rate, frequency, residue, block_len):
    damping = 0.125 * decay_rate
    turning = 0.125 * frequency
    scaling = jnp.sqrt(2.0 * damping)
    coef_re = scaling * residue[0]
    coef_im = scaling * residue[1]
    offsets = jnp.arange(block_len).astype(jnp.float32)

    def powers(counts):
        fading = jnp.exp(-damping[None] * counts[:, None, None])
        phase = turning[None] * counts[:, None, None]
        return (fading * jnp.cos(phase), fading * jnp.sin(phase))

    back_re, back_im = powers(block_len - 1.0 - offsets)
    ahead_re, ahead_im = powers(offsets + 1.0)
    out_re, out_im = cmul(coef_re[None], coef_im[None], ahead_re, ahead_im)
    lag_re, lag_im = powers(offsets)
    filt = jnp.sum(coef_re[None] * lag_re - coef_im[None] * lag_im, axis=1)
    places = jnp.arange(block_len)
    differ = places[:, None] - places[None, :]
    picked = jnp.take(filt, jnp.maximum(differ, 0), axis=0)
    toeplitz = jnp.where((differ >= 0)[:, :, None], picked, jnp.zeros_like(picked))
    jump_re, jump_im = powers(jnp.full((1,), block_len).astype(jnp.float32))
    return (back_re, back_im, out_re, out_im, toeplitz, jump_re[0], jump_im[0])


def chain(earlier, later):
    sum_re, sum_im = cmul(earlier[0], earlier[1], later[2], later[3])
    pow_re, pow_im = cmul(earlier[2], earlier[3], later[2], later[3])
    return (sum_re + later[0], sum_im + later[1], pow_re, pow_im)


def on_device(
    gate_input, key_input, value_input, decay_rate, frequency, residue, skip_gain, out_weight
):
    highest = lax.Precision.HIGHEST
    signal = key_input.astype(jnp.float32) * value_input.astype(jnp.float32)
    tok_len, chans = signal.shape
    block_len = 16
    block_count = tok_len // block_len
    back_re, back_im, out_re, out_im, toeplitz, jump_re, jump_im = filter_tables(
        decay_rate, frequency, residue, block_len
    )
    blocks = signal.reshape(block_count, block_len, chans)
    entry_re = jnp.einsum("snc,bsc->bnc", back_re, blocks, precision=highest)
    entry_im = jnp.einsum("snc,bsc->bnc", back_im, blocks, precision=highest)

    def advance(state, entry):
        moved_re, moved_im = cmul(jump_re, jump_im, state[0], state[1])
        grown_re, grown_im = cmul(state[2], state[3], jump_re, jump_im)
        return ((moved_re + entry[0], moved_im + entry[1], grown_re, grown_im), state)

    zeros = jnp.zeros(jump_re.shape, jnp.float32)
    ones = jnp.ones(jump_re.shape, jnp.float32)
    final, starts = lax.scan(advance, (zeros, zeros, ones, zeros), (entry_re, entry_im))
    local_re, local_im, device_re, device_im = final
    prefix = entering(
        (local_re, local_im, device_re, device_im), "ctx", chain, (zeros, zeros, ones, zeros)
    )
    incoming_re, incoming_im = (prefix[0], prefix[1])
    carried_re, carried_im = cmul(starts[2], starts[3], incoming_re[None], incoming_im[None])
    begin_re = starts[0] + carried_re
    begin_im = starts[1] + carried_im
    far = jnp.einsum("tnc,bnc->btc", out_re, begin_re, precision=highest) - jnp.einsum(
        "tnc,bnc->btc", out_im, begin_im, precision=highest
    )
    near = jnp.einsum("tsc,bsc->btc", toeplitz, blocks, precision=highest)
    conv = (near + far).reshape(tok_len, chans)
    gated = (gate_input.astype(jnp.float32) * (conv + skip_gain[None, :] * signal)).astype(
        jnp.bfloat16
    )
    whole = lax.all_gather(gated, "ch", axis=1, tiled=True)
    all_rows = lax.all_gather(out_weight, "ctx", axis=0, tiled=True)
    mixed = jnp.dot(whole, all_rows, preferred_element_type=jnp.float32)
    return mixed.astype(jnp.bfloat16)


def solution(mesh):
    placed = (
        P("ctx", "ch"),
        P("ctx", "ch"),
        P("ctx", "ch"),
        P(None, "ch"),
        P(None, "ch"),
        P(None, None, "ch"),
        P("ch"),
        P("ctx", "ch"),
    )
    return jax.shard_map(
        on_device, mesh=mesh, in_specs=placed, out_specs=P("ctx", "ch"), check_vma=False
    )
```

profile of v0, /device:TPU:8, one launch (start us, length us, event | category | flops | bytes accessed | tf_op | source)
XLA Modules:
  0.0 906.5 jit_solution(10265172625318404622)
XLA Ops:
  6.6 1.1 convert_multiply_fusion
  7.7 3.7 copy.51
  11.5 6.1 multiply_add_fusion.1
  17.6 4.1 copy.54
  21.8 9.9 %convolution_bitcast_fusion.1 = f32[16,16,512]{1,0,2:T(8,128)} fusion(f32[16,16,512]{1,0,2:T(8,128)} %copy.51, f32[16,16,512]{1,0,2:T(8,128)} %copy.54), kind=kOutput, calls=%fused_computation.21 | convolution fusion | flops 25165824 | bytes 1572864 | tf_op jit(solution)/shard_map/snc,bsc->bnc/dot_general | solution.py:69
  31.7 3.5 copy.57
  35.2 3.7 copy.56
  38.9 9.9 %convolution_bitcast_fusion = f32[16,16,512]{1,0,2:T(8,128)} fusion(f32[16,16,512]{1,0,2:T(8,128)} %copy.51, f32[16,16,512]{1,0,2:T(8,128)} %copy.56), kind=kOutput, calls=%fused_computation.20 | convolution fusion | flops 25165824 | bytes 1572864 | tf_op jit(solution)/shard_map/snc,bsc->bnc/dot_general | solution.py:70
  48.8 3.5 copy.58
  52.5 14.0 %while.41 = (s32[]{:T(128)}, f32[16,512]{1,0:T(8,128)S(1)}, f32[16,512]{1,0:T(8,128)S(1)}, f32[16,512]{1,0:T(8,128)S(1)}, f32[16,512]{1,0:T(8,128)S(1)}, /*index...) while((s32[]{:T(128)}, f32[16,512]{1,0:T(8,128)S(1)}, ...), condition=%wide.region_2.3_spmd.clone, body=%wide.region_1.2_spmd.clone.sunk | while | flops 180227 | bytes 655533 | solution.py:79
  69.6 1.8 gather_fusion
  71.4 2.0 select_select_fusion
  73.4 4.5 copy.52
  77.9 3.6 copy.60
  81.5 3.7 copy.62
  85.2 12.3 %fusion.17 = f32[512,16,16]{2,1,0:T(8,128)} fusion(f32[16,16,512]{1,0,2:T(8,128)} %copy.51, f32[16,16,512]{1,0,2:T(8,128)} %copy.52), kind=kOutput, calls=%fused_computation.66 | convolution fusion | flops 25165824 | bytes 1572864 | tf_op jit(solution)/shard_map/tsc,bsc->btc/dot_general | solution.py:91
  97.5 115.2 %all-gather.15.cloned.1.call-done = f32[1024,512]{1,0:T(8,128)} async-done(((f32[16,512]{1,0:T(8,128)}), f32[1024,512]{1,0:T(8,128)}) %all-gather.15.cloned.1.call-update) | async-done | bytes 2097168 | tf_op jit(solution)/shard_map/all_gather | solution.py:9
  212.7 139.9 %all-gather.17.cloned.1.call-done = f32[1024,512]{1,0:T(8,128)} async-done(((f32[16,512]{1,0:T(8,128)}), f32[1024,512]{1,0:T(8,128)}) %all-gather.17.cloned.1.call-update) | async-done | bytes 2097168 | tf_op jit(solution)/shard_map/all_gather | solution.py:9
  352.6 139.9 %all-gather.19.cloned.1.call-done = f32[1024,512]{1,0:T(8,128)} async-done(((f32[16,512]{1,0:T(8,128)}), f32[1024,512]{1,0:T(8,128)}) %all-gather.19.cloned.1.call-update) | async-done | bytes 2097168 | tf_op jit(solution)/shard_map/all_gather | solution.py:9
  492.5 139.8 %all-gather.21.cloned.1.call-done = f32[1024,512]{1,0:T(8,128)} async-done(((f32[16,512]{1,0:T(8,128)}), f32[1024,512]{1,0:T(8,128)}) %all-gather.21.cloned.1.call-update) | async-done | bytes 2097168 | tf_op jit(solution)/shard_map/all_gather | solution.py:9
  632.3 54.2 %while.42 = (s32[]{:T(128)}, f32[16,512]{1,0:T(8,128)S(1)}, f32[16,512]{1,0:T(8,128)S(1)}, s32[]{:T(128)}, f32[64,16,512]{2,1,0:T(8,128)}, /*index=5*/f32[64,16,...) while((s32[]{:T(128)}, f32[16,512]{1,0:T(8,128)S(1)}, ...), condition=%wide.region_4.5_spmd.clone, body=%wide.region_3.4_spmd.clone.sunk | while | flops 98308 | bytes 262277 | solution.py:18
  643.5 0.9 fusion.32
  644.3 0.8 fusion.32
  645.2 0.8 fusion.32
  646.1 0.8 fusion.32
  646.9 0.8 fusion.32
  647.8 0.8 fusion.32
  648.6 0.8 fusion.32
  649.5 0.8 fusion.32
  650.4 0.8 fusion.32
  651.2 0.8 fusion.32
  652.1 0.8 fusion.32
  652.9 0.8 fusion.32
  653.8 0.8 fusion.32
  654.7 0.8 fusion.32
  655.5 0.8 fusion.32
  656.4 0.8 fusion.32
  657.2 0.8 fusion.32
  658.1 0.8 fusion.32
  686.8 3.7 copy.59
  690.4 3.6 copy.61
  694.1 9.5 %fusion.18 = f32[512,16,16]{2,1,0:T(8,128)S(1)} fusion(f32[16,16,512]{1,0,2:T(8,128)} %copy.59, f32[16,16,512]{1,0,2:T(8,128)} %copy.60), kind=kOutput, calls=%fused_computation.67 | convolution fusion | flops 25165824 | bytes 1572864 | tf_op jit(solution)/shard_map/tnc,bnc->btc/dot_general | solution.py:88
  703.6 8.5 add_bitcast_fusion
  712.1 2.9 copy.63
  715.0 0.8 fusion.15
  716.5 27.5 %all-gather.11.cloned.1.call-done = bf16[256,4096]{1,0:T(8,128)(2,1)} async-done(((bf16[256,512]{1,0:T(8,128)(2,1)}), bf16[256,4096]{1,0:T(8,128)(2,1)}) %all-gather.11.cloned.1.call-update) | async-done | bytes 2097168 | tf_op jit(solution)/shard_map/all_gather | solution.py:96
  744.0 150.7 %all-gather.13.cloned.1.call-done = bf16[4096,512]{1,0:T(8,128)(2,1)} async-done(((bf16[64,512]{1,0:T(8,128)(2,1)}), bf16[4096,512]{1,0:T(8,128)(2,1)}) %all-gather.13.cloned.1.call-update) | async-done | bytes 4194320 | tf_op jit(solution)/shard_map/all_gather | solution.py:97
  894.6 4.8 convolution_convert_fusion
  (151 shorter events, 55.3 us)
Async XLA Ops:
  6.5 4.8 copy-start.11
  6.5 4.8 copy-start.12
  6.5 4.8 copy-start.10
  6.5 206.1 %all-gather.15.cloned.1.call-start = ((), (), s32[]{:S(2)}) async-start(), calls=%async_computation.2 | async-start | bytes 2129920 | tf_op jit(solution)/shard_map/all_gather | solution.py:9
  66.5 0.6 copy-start.5
  66.6 0.7 copy-start.6
  66.6 1.4 copy-start.3
  66.6 2.1 copy-start.4
  67.2 285.4 %all-gather.17.cloned.1.call-start = ((), (), s32[]{:S(2)}) async-start(), calls=%async_computation.3 | async-start | bytes 2129920 | tf_op jit(solution)/shard_map/all_gather | solution.py:9
  67.9 424.6 %all-gather.19.cloned.1.call-start = ((), (), s32[]{:S(2)}) async-start(), calls=%async_computation.4 | async-start | bytes 2129920 | tf_op jit(solution)/shard_map/all_gather | solution.py:9
  68.7 563.6 %all-gather.21.cloned.1.call-start = ((), (), s32[]{:S(2)}) async-start(), calls=%async_computation.5 | async-start | bytes 2129920 | tf_op jit(solution)/shard_map/all_gather | solution.py:9
  69.2 674.7 %all-gather.11.cloned.1.call-start = ((), (), s32[]{:S(2)}) async-start(), calls=%async_computation | async-start | bytes 2359296 | tf_op jit(solution)/shard_map/all_gather | solution.py:96
  694.1 9.5 %copy-start = (f32[512,16,16]{2,1,0:T(8,128)S(1)}, f32[512,16,16]{2,1,0:T(8,128)}, u32[]{:S(2)}) copy-start(f32[512,16,16]{2,1,0:T(8,128)} %fusion.17) | copy-start | bytes 1572868
  694.1 9.5 %copy-start.1 = (f32[16,16,512]{1,0,2:T(8,128)S(1)}, f32[16,16,512]{1,0,2:T(8,128)}, u32[]{:S(2)}) copy-start(f32[16,16,512]{1,0,2:T(8,128)} %copy.62) | copy-start | bytes 1572868
  694.1 9.5 %copy-start.2 = (f32[16,16,512]{1,0,2:T(8,128)S(1)}, f32[16,16,512]{1,0,2:T(8,128)}, u32[]{:S(2)}) copy-start(f32[16,16,512]{1,0,2:T(8,128)} %copy.61) | copy-start | bytes 1572868
  712.1 2.9 copy-start.7
  712.1 2.9 copy-start.8
  712.1 2.9 copy-start.9
  712.1 2.9 copy-start.13
  715.9 178.7 %all-gather.13.cloned.1.call-start = ((), (), s32[]{:S(2)}) async-start(), calls=%async_computation.1 | async-start | bytes 4259840 | tf_op jit(solution)/shard_map/all_gather | solution.py:97
Sparse Core Ops, SparseCore 0:
  67.3 145.3 all-gather.14
  215.6 136.9 all-gather.16
  355.5 136.9 all-gather.18
  495.3 136.9 all-gather.20
  716.0 27.8 all-gather.10
  746.8 147.8 all-gather.12
where the time goes:
time: 918 us; the launch traced here: 906 us
  waiting for transfers between devices  715 us (78%)
  other arithmetic  76.7 us (8%)
  matrix products  54.8 us (6%)
  local copies, waits for them, and re-layouts  43.3 us (5%)
  between operations  14 us (2%)
    all_gather x4, waiting for transfers between devices, entering(): pieces = jax.tree.map(lambda part: lax.all_gather(part, axis), value)  535 us
    all_gather x1, waiting for transfers between devices, on_device(): all_rows = lax.all_gather(out_weight, 'ctx', axis=0, tiled=True)  151 us
    select_n x63, other arithmetic, hop(): jnp.where(position < mine, new, old)  52.8 us
    all_gather x1, waiting for transfers between devices, on_device(): whole = lax.all_gather(gated, 'ch', axis=1, tiled=True)  27.5 us
    add x17, other arithmetic, cmul(): return (a_re * b_re - a_im * b_im, a_re * b_im + a_im * b_re)  19.1 us
  transfers between devices with their start and end apart: 6, of which 6 were waited for; matrix products, arithmetic and copies ran while one was open for 3% of the time, Pallas kernels for 0%

commit v1 on v0

--- a/solution.py
+++ b/solution.py
@@ -2,6 +2,28 @@
 import jax.numpy as jnp
 from jax import lax
 from jax.sharding import PartitionSpec as P
+
+
+def _match_classes(x_in, d_out):
+    z2 = list(x_in.shape[1:])
+    z2[d_out] *= x_in.shape[0]
+    return jnp.moveaxis(x_in, 0, d_out).reshape(z2)
+
+
+def entries_create(view, named_axis, at_axis):
+    workers = lax.psum(1, named_axis)
+    rack = [(t, (t + 1) % workers) for t in range(workers)]
+    crops = [(b, pp) for pp, b in rack]
+    a_next, w1 = ([], [])
+    for jj in range(workers - 1):
+        if jj % 2 == 0:
+            a_next.append(lax.ppermute(a_next[-1] if a_next else view, named_axis, rack))
+        else:
+            w1.append(lax.ppermute(w1[-1] if w1 else view, named_axis, crops))
+    newest = jnp.stack([*a_next[::-1], view, *w1])
+    o_now = lax.axis_index(named_axis) - len(a_next)
+    newest = newest[(jnp.arange(workers) - o_now) % workers]
+    return _match_classes(newest, at_axis)
 
 
 def entering(value, axis, join, neutral):
@@ -93,7 +115,7 @@
     gated = (gate_input.astype(jnp.float32) * (conv + skip_gain[None, :] * signal)).astype(
         jnp.bfloat16
     )
-    whole = lax.all_gather(gated, "ch", axis=1, tiled=True)
+    whole = entries_create(gated, "ch", 1)
     all_rows = lax.all_gather(out_weight, "ctx", axis=0, tiled=True)
     mixed = jnp.dot(whole, all_rows, preferred_element_type=jnp.float32)
     return mixed.astype(jnp.bfloat16)

time: 918 us -> 801 us (0.87)
  waiting for transfers between devices: 715 us -> 582 us
  local copies, waits for them, and re-layouts: 43.3 us -> 53.8 us
    all_gather x1, waiting for transfers between devices: 151 us -> 28.2 us  [on_device(): all_rows = lax.all_gather(out_weight, 'ctx', axis=0, tiled=True)]
    all_gather x1 -> x0, waiting for transfers between devices: 27.5 us -> none  [on_device(): whole = lax.all_gather(gated, 'ch', axis=1, tiled=True)]
    ppermute x0 -> x7, waiting for transfers between devices: none -> 17 us  [the longest x4 16.7 us: entries_create(): lax.ppermute(a_next[-1] if a_next else view, named_axis, rack)]
  transfers between devices with their start and end apart: 6 -> 12, of which waited for: 6 -> 10; matrix products, arithmetic and copies ran while one was open for 3% -> 15% of each run, Pallas kernels for 0% -> 0%
where the time goes in v1:
time: 801 us; the launch traced here: 789 us
  waiting for transfers between devices  582 us (73%)
  other arithmetic  76.1 us (10%)
  matrix products  54.8 us (7%)
  local copies, waits for them, and re-layouts  53.8 us (7%)
  between operations  13.7 us (2%)
    all_gather x4, waiting for transfers between devices, entering(): pieces = jax.tree.map(lambda part: lax.all_gather(part, axis), value)  534 us
    select_n x63, other arithmetic, hop(): jnp.where(position < mine, new, old)  52.8 us
    all_gather x1, waiting for transfers between devices, on_device(): all_rows = lax.all_gather(out_weight, 'ctx', axis=0, tiled=True)  28.2 us
    add x17, other arithmetic, cmul(): return (a_re * b_re - a_im * b_im, a_re * b_im + a_im * b_re)  19.1 us
    ppermute x4, waiting for transfers between devices, entries_create(): lax.ppermute(a_next[-1] if a_next else view, named_axis, rack)  16.7 us
  transfers between devices with their start and end apart: 12, of which 10 were waited for; matrix products, arithmetic and copies ran while one was open for 15% of the time, Pallas kernels for 0%

profile of v1, /device:TPU:8, one launch (start us, length us, event | category | flops | bytes accessed | tf_op | source)
XLA Modules:
  0.0 788.7 jit_solution(7902737293759218759)
XLA Ops:
  6.6 1.1 convert_multiply_fusion
  7.7 3.7 copy.53
  11.6 6.1 multiply_add_fusion.1
  17.7 4.1 copy.56
  21.8 9.9 %convolution_bitcast_fusion.1 = f32[16,16,512]{1,0,2:T(8,128)} fusion(f32[16,16,512]{1,0,2:T(8,128)} %copy.53, f32[16,16,512]{1,0,2:T(8,128)} %copy.56), kind=kOutput, calls=%fused_computation.22 | convolution fusion | flops 25165824 | bytes 1572864 | tf_op jit(solution)/shard_map/snc,bsc->bnc/dot_general | solution.py:91
  31.7 3.5 copy.59
  35.2 3.7 copy.58
  38.9 9.8 %convolution_bitcast_fusion = f32[16,16,512]{1,0,2:T(8,128)} fusion(f32[16,16,512]{1,0,2:T(8,128)} %copy.53, f32[16,16,512]{1,0,2:T(8,128)} %copy.58), kind=kOutput, calls=%fused_computation.21 | convolution fusion | flops 25165824 | bytes 1572864 | tf_op jit(solution)/shard_map/snc,bsc->bnc/dot_general | solution.py:92
  48.7 3.5 copy.60
  52.5 14.0 %while.41 = (s32[]{:T(128)}, f32[16,512]{1,0:T(8,128)S(1)}, f32[16,512]{1,0:T(8,128)S(1)}, f32[16,512]{1,0:T(8,128)S(1)}, f32[16,512]{1,0:T(8,128)S(1)}, /*index...) while((s32[]{:T(128)}, f32[16,512]{1,0:T(8,128)S(1)}, ...), condition=%wide.region_2.3_spmd.clone, body=%wide.region_1.2_spmd.clone.sunk | while | flops 180227 | bytes 655533 | solution.py:101
  69.9 1.8 gather_fusion
  71.7 2.0 select_select_fusion
  73.7 4.5 copy.54
  78.2 12.3 %fusion.19 = f32[512,16,16]{2,1,0:T(8,128)} fusion(f32[16,16,512]{1,0,2:T(8,128)} %copy.53, f32[16,16,512]{1,0,2:T(8,128)} %copy.54), kind=kOutput, calls=%fused_computation.82 | convolution fusion | flops 25165824 | bytes 1572864 | tf_op jit(solution)/shard_map/tsc,bsc->btc/dot_general | solution.py:113
  90.5 3.6 copy.62
  94.1 3.7 copy.64
  97.8 114.8 %all-gather.12.cloned.1.call-done = f32[1024,512]{1,0:T(8,128)} async-done(((f32[16,512]{1,0:T(8,128)}), f32[1024,512]{1,0:T(8,128)}) %all-gather.12.cloned.1.call-update) | async-done | bytes 2097168 | tf_op jit(solution)/shard_map/all_gather | solution.py:31
  212.6 139.9 %all-gather.14.cloned.1.call-done = f32[1024,512]{1,0:T(8,128)} async-done(((f32[16,512]{1,0:T(8,128)}), f32[1024,512]{1,0:T(8,128)}) %all-gather.14.cloned.1.call-update) | async-done | bytes 2097168 | tf_op jit(solution)/shard_map/all_gather | solution.py:31
  352.5 139.9 %all-gather.16.cloned.1.call-done = f32[1024,512]{1,0:T(8,128)} async-done(((f32[16,512]{1,0:T(8,128)}), f32[1024,512]{1,0:T(8,128)}) %all-gather.16.cloned.1.call-update) | async-done | bytes 2097168 | tf_op jit(solution)/shard_map/all_gather | solution.py:31
  492.5 139.8 %all-gather.18.cloned.1.call-done = f32[1024,512]{1,0:T(8,128)} async-done(((f32[16,512]{1,0:T(8,128)}), f32[1024,512]{1,0:T(8,128)}) %all-gather.18.cloned.1.call-update) | async-done | bytes 2097168 | tf_op jit(solution)/shard_map/all_gather | solution.py:31
  632.2 54.2 %while.42 = (s32[]{:T(128)}, f32[16,512]{1,0:T(8,128)S(1)}, f32[16,512]{1,0:T(8,128)S(1)}, s32[]{:T(128)}, f32[64,16,512]{2,1,0:T(8,128)}, /*index=5*/f32[64,16,...) while((s32[]{:T(128)}, f32[16,512]{1,0:T(8,128)S(1)}, ...), condition=%wide.region_4.5_spmd.clone, body=%wide.region_3.4_spmd.clone.sunk | while | flops 98308 | bytes 262277 | solution.py:40
  633.1 0.8 fusion.34
  633.9 0.8 fusion.34
  653.7 0.8 fusion.34
  658.0 0.8 fusion.34
  661.5 0.8 fusion.34
  664.9 0.8 fusion.34
  667.5 0.8 fusion.34
  668.4 0.8 fusion.34
  672.7 0.8 fusion.34
  675.2 0.8 fusion.34
  683.0 0.8 fusion.34
  686.7 3.7 copy.61
  690.4 3.6 copy.63
  694.1 9.5 %fusion.20 = f32[512,16,16]{2,1,0:T(8,128)S(1)} fusion(f32[16,16,512]{1,0,2:T(8,128)} %copy.61, f32[16,16,512]{1,0,2:T(8,128)} %copy.62), kind=kOutput, calls=%fused_computation.83 | convolution fusion | flops 25165824 | bytes 1572864 | tf_op jit(solution)/shard_map/tnc,bnc->btc/dot_general | solution.py:110
  703.6 8.6 %add_bitcast_fusion = f32[16,16,512]{1,0,2:T(8,128)} fusion(f32[512,16,16]{2,1,0:T(8,128)S(1)} %copy-done, f32[512,16,16]{2,1,0:T(8,128)S(1)} %fusion.20, f32[16,16,512]{1,0,2:T(8,128)S(1)} %copy-done.2, f32[16,16,512]{1,0,2:T(8,128)S(1)} %copy-done.1), kind=kOutput, calls=%fused_computation.20 | convolution fusion | flops 25427968 | bytes 2621440 | tf_op jit(solution)/shard_map/tnc,bnc->btc/dot_general | solution.py:110
  712.1 2.9 copy.65
  715.2 5.8 collective-permute-done
  721.0 1.7 collective-permute-start.4
  722.8 4.1 collective-permute-done.1
  726.8 2.1 collective-permute-start.5
  729.0 3.7 collective-permute-done.2
  732.9 2.3 collective-permute-start.6
  735.2 3.3 collective-permute-done.3
  744.2 2.3 gather_fusion.1
  746.5 2.4 copy.66
  748.9 28.2 %all-gather.10.cloned.1.call-done = bf16[4096,512]{1,0:T(8,128)(2,1)} async-done(((bf16[64,512]{1,0:T(8,128)(2,1)}), bf16[4096,512]{1,0:T(8,128)(2,1)}) %all-gather.10.cloned.1.call-update) | async-done | bytes 4194320 | tf_op jit(solution)/shard_map/all_gather | solution.py:119
  777.2 4.8 convolution_convert_fusion
  (174 shorter events, 67.2 us)
Async XLA Ops:
  6.5 4.9 copy-start.11
  6.5 4.9 copy-start.12
  6.5 4.9 copy-start.10
  6.5 206.1 %all-gather.12.cloned.1.call-start = ((), (), s32[]{:S(2)}) async-start(), calls=%async_computation.1 | async-start | bytes 2129920 | tf_op jit(solution)/shard_map/all_gather | solution.py:31
  66.5 0.6 copy-start.5
  66.5 0.7 copy-start.6
  66.5 1.4 copy-start.3
  66.5 2.1 copy-start.4
  67.1 285.4 %all-gather.14.cloned.1.call-start = ((), (), s32[]{:S(2)}) async-start(), calls=%async_computation.2 | async-start | bytes 2129920 | tf_op jit(solution)/shard_map/all_gather | solution.py:31
  67.9 424.6 %all-gather.16.cloned.1.call-start = ((), (), s32[]{:S(2)}) async-start(), calls=%async_computation.3 | async-start | bytes 2129920 | tf_op jit(solution)/shard_map/all_gather | solution.py:31
  68.6 563.6 %all-gather.18.cloned.1.call-start = ((), (), s32[]{:S(2)}) async-start(), calls=%async_computation.4 | async-start | bytes 2129920 | tf_op jit(solution)/shard_map/all_gather | solution.py:31
  69.2 708.0 %all-gather.10.cloned.1.call-start = ((), (), s32[]{:S(2)}) async-start(), calls=%async_computation | async-start | bytes 4259840 | tf_op jit(solution)/shard_map/all_gather | solution.py:119
  694.1 9.5 %copy-start = (f32[512,16,16]{2,1,0:T(8,128)S(1)}, f32[512,16,16]{2,1,0:T(8,128)}, u32[]{:S(2)}) copy-start(f32[512,16,16]{2,1,0:T(8,128)} %fusion.19) | copy-start | bytes 1572868
  694.1 9.5 %copy-start.1 = (f32[16,16,512]{1,0,2:T(8,128)S(1)}, f32[16,16,512]{1,0,2:T(8,128)}, u32[]{:S(2)}) copy-start(f32[16,16,512]{1,0,2:T(8,128)} %copy.64) | copy-start | bytes 1572868
  694.1 9.5 %copy-start.2 = (f32[16,16,512]{1,0,2:T(8,128)S(1)}, f32[16,16,512]{1,0,2:T(8,128)}, u32[]{:S(2)}) copy-start(f32[16,16,512]{1,0,2:T(8,128)} %copy.63) | copy-start | bytes 1572868
  712.1 2.9 copy-start.7
  712.1 2.9 copy-start.8
  712.1 2.9 copy-start.9
  712.1 2.9 copy-start.13
  715.2 5.8 collective-permute-start
  721.0 5.8 collective-permute-start.1
  721.0 5.8 collective-permute-start.4
  726.8 5.8 collective-permute-start.2
  726.8 6.0 collective-permute-start.5
  732.6 5.8 collective-permute-start.3
  732.9 10.7 %collective-permute-start.6 = (bf16[256,512]{1,0:T(8,128)(2,1)S(1)}, bf16[256,512]{1,0:T(8,128)(2,1)S(1)}, u32[]{:S(2)}, u32[]{:S(2)}) collective-permute-start(bf16[256,512]{1,0:T(8,128)(2,1)S(1)} %collective-permute-done.5), channel_id=1, source_target_pairs={{1,0},{2,1},{3,2},{4,3},{5,4},{6,5},{7,6},{0,7},{9,8},{10,9},{11,1... | collective-permute-start | bytes 786440 | tf_op jit(solution)/shard_map/ppermute | solution.py:22
Sparse Core Ops, SparseCore 0:
  67.2 145.3 all-gather.11
  215.5 136.9 all-gather.13
  355.5 136.9 all-gather.15
  495.3 136.9 all-gather.17
  635.0 142.0 all-gather.9
